TPU v7x, 256 devices: a whole 4x4x8 slice. The times are simulated.
256 devices in a mesh: row: 16 (over x_lo, y, core), col: 16 (over z, x_hi).
Axes of the slice: x: 4 (x_hi: 2, x_lo: 2; x = x_hi * 2 + x_lo), y: 4, z: 8, core: 2. Of those that a mesh axis runs over, the one named last changes fastest.
Arguments:
- adj_values: bfloat16 [2, 16, 16, 20, 128, 128], P(None, 'row', 'col'), may hold values from -6 to 6
- block_rows: int32 [2, 16, 16, 20], P(None, 'row', 'col'), may hold values from 0 to 47, as said below
- block_cols: int32 [2, 16, 16, 20], P(None, 'row', 'col'), may hold values from 0 to 15, as said below
- block_counts: int32 [2, 16, 16], P(None, 'row', 'col'), may hold values from 5 to 20, as said below
- block_scales: bfloat16 [2, 16, 16, 20], P(None, 'row', 'col'), may hold values from 0.0049743652 to 0.049804688
- panel_features: bfloat16 [2, 256, 32768], P(None, 'col', 'row'), may hold values from -6 to 6
- weight: bfloat16 [256, 256], replicated, may hold values from -0.375 to 0.375
- out_bias: float32 [256], replicated, may hold values from -3 to 3
Outputs:
- layer_out: bfloat16 [98304, 256], P(('row', 'col'))
Inputs may be any that keep to these rules, and one draw needn't show every extreme that they name: `block_rows`: block rows are local to the 48 block rows of a row index. The slots of one device in one panel name distinct (block row, block column) pairs. `block_cols`: block columns index the 16 block columns of a col index's part of the panel. `block_counts`: in every panel, all devices of at least one row index hold exactly 20 live blocks.
All inputs are finite; a program needn't handle non-finite values.
Results may differ from a plain program's by a relative error of at most 0.0044.
Values may be sent and summed in bfloat16 or wider, within the bound.
No kernel may reach another device: no remote copies, remote signals or barrier semaphores. Data moves between devices by JAX's collectives and lax.ppermute only.
A program may use at most 64 MiB of HBM per device.

v0:
```python
import jax
import jax.numpy as jnp
from jax import lax
from jax.sharding import Mesh
from jax.sharding import PartitionSpec as P

ROWB_DEV = 48
PCB = 16
COL = ("col_0", "col_1")
ROW_COL = ("row", "col_0", "col_1")


def in_blocks(x, dim, peers):
    before, after = (x.shape[:dim], x.shape[dim + 1 :])
    return jnp.moveaxis(x.reshape(*before, peers, -1, *after), dim, 0)


def edges_of(length, count):
    hop = length // count
    if hop >= 8:
        hop -= hop % 8
    return [hop * k for k in range(1, count)]


def in_order(tiles, dim):
    tiles = jnp.moveaxis(tiles, 0, dim)
    lengths = tiles.shape
    return tiles.reshape(*lengths[:dim], lengths[dim] * lengths[dim + 1], *lengths[dim + 2 :])


def several_exchanges(x, axis, pieces, split_dim, concat_dim):
    tiles = in_blocks(x, split_dim, lax.axis_size(axis))
    widest = max(range(1, max(2, tiles.ndim - 1)), key=lambda d: tiles.shape[d])
    finished = []
    for share in jnp.split(tiles, edges_of(tiles.shape[widest], pieces), axis=widest):
        if share.size:
            finished.append(lax.all_to_all(share, axis, split_axis=0, concat_axis=0, tiled=True))
    return in_order(jnp.concatenate(finished, axis=widest), concat_dim)


def scatter_axes(x, axes, dim):
    for axis in axes:
        x = lax.psum_scatter(x, axis, scatter_dimension=dim, tiled=True)
    return x


def spread_rows(running, values, feature_cols, row_ids, live_scale):
    contrib = jnp.einsum("bfk,brk->bfr", feature_cols, values, preferred_element_type=jnp.float32)
    return running.at[row_ids].add(contrib * live_scale[:, None, None])


def body(
    adj_values, block_rows, block_cols, block_counts, block_scales, panel_features, weight, out_bias
):
    nsteps = adj_values.shape[0]
    blocksz = adj_values.shape[4]
    feat_all = weight.shape[0]
    out_width = weight.shape[1]
    rows_here = ROWB_DEV * blocksz // lax.axis_size(COL)
    panels = lax.all_gather(panel_features, "row", axis=2, tiled=True)
    shares = several_exchanges(panels, COL, 2, 2, 1)
    share_blocks = shares.reshape(nsteps, feat_all, PCB, blocksz).transpose(0, 2, 1, 3)
    running = jnp.zeros((ROWB_DEV, feat_all, blocksz), jnp.float32)
    slot_ids = jnp.arange(adj_values.shape[3], dtype=jnp.int32)
    for step in range(nsteps):
        live_scale = jnp.where(
            slot_ids < block_counts[step, 0, 0], block_scales[step, 0, 0].astype(jnp.float32), 0.0
        )
        feature_cols = share_blocks[step][block_cols[step, 0, 0]]
        running = spread_rows(
            running, adj_values[step, 0, 0], feature_cols, block_rows[step, 0, 0], live_scale
        )
    summed = scatter_axes(running, COL, 0)
    aggregate = summed.astype(jnp.bfloat16)
    before = jnp.einsum(
        "zfr,fg->zrg", aggregate, weight, preferred_element_type=jnp.float32
    ).reshape(rows_here, out_width)
    return jax.nn.relu(before + out_bias).astype(jnp.bfloat16)


def solution(mesh):
    split = Mesh(mesh.devices.reshape(mesh.shape["row"], 8, 2), ("row", "col_0", "col_1"))
    in_specs = (
        P(None, "row", COL, None, None, None),
        P(None, "row", COL, None),
        P(None, "row", COL, None),
        P(None, "row", COL),
        P(None, "row", COL, None),
        P(None, COL, "row"),
        P(),
        P(),
    )
    out_specs = P(ROW_COL, None)
    return jax.shard_map(body, mesh=split, in_specs=in_specs, out_specs=out_specs, check_vma=False)
```

profile of v0, /device:TPU:1, one launch (start us, length us, event | category | flops | bytes accessed | tf_op | source)
XLA Modules:
  0.0 258.9 jit_solution(18103866229574193103)
XLA Ops:
  6.5 0.7 all-gather.2.cloned.1.call-update
  7.3 42.4 %all-gather.2.cloned.1.call-done = bf16[2,16,32768]{2,1,0:T(8,128)(2,1)} async-done(((bf16[2,16,2048]{2,1,0:T(8,128)(2,1)}), bf16[2,16,32768]{2,1,0:T(8,128)(2,1)}) %all-gather.2.cloned.1.call-update) | async-done | bytes 2097168 | tf_op jit(solution)/shard_map/all_gather | solution.py:60
  49.6 2.7 %copy.21 = bf16[4,8,16,2048]{3,2,1,0:T(8,128)(2,1)S(1)} copy(bf16[4,8,16,2048]{3,1,2,0:T(8,128)(2,1)} %bitcast.67) | data formatting | bytes 4194304
  52.4 0.2 bitcast_bitcast_fusion
  52.6 0.1 fusion.13
  52.8 1.6 copy.15
  54.4 8.9 %all-to-all-start = ((bf16[16,2,8,2048]{3,2,1,0:T(8,128)(2,1)}), bf16[16,2,8,2048]{3,2,1,0:T(8,128)(2,1)S(1)}, u32[]{:S(2)}, u32[]{:S(2)}) async-start(bf16[16,2,8,2048]{3,2,1,0:T(8,128)(2,1)} %copy.15), calls=%async_computation | async-start | bytes 2097152 | tf_op jit(solution)/shard_map/all_to_all | solution.py:37
  63.3 1.6 copy.16
  64.9 25.6 %all-to-all-done = bf16[16,2,8,2048]{3,2,1,0:T(8,128)(2,1)S(1)} async-done(((bf16[16,2,8,2048]{3,2,1,0:T(8,128)(2,1)}), bf16[16,2,8,2048]{3,2,1,0:T(8,128)(2,1)S(1)}, u32[]{:S(2)}, u32[]{:S(2)}) %all-to-all-start) | async-done | bytes 1048608 | tf_op jit(solution)/shard_map/all_to_all | solution.py:37
  90.5 5.9 %all-to-all-start.1 = ((bf16[16,2,8,2048]{3,2,1,0:T(8,128)(2,1)}), bf16[16,2,8,2048]{3,2,1,0:T(8,128)(2,1)S(1)}, u32[]{:S(2)}, u32[]{:S(2)}) async-start(bf16[16,2,8,2048]{3,2,1,0:T(8,128)(2,1)} %copy.16), calls=%async_computation.1 | async-start | bytes 2097152 | tf_op jit(solution)/shard_map/all_to_all | solution.py:37
  96.5 0.0 reduce-scatter.3.cloned.1.call-start
  96.5 0.6 fusion.14
  97.1 1.8 compare_select_fusion.4
  99.0 23.6 %all-to-all-done.1 = bf16[16,2,8,2048]{3,2,1,0:T(8,128)(2,1)S(1)} async-done(((bf16[16,2,8,2048]{3,2,1,0:T(8,128)(2,1)}), bf16[16,2,8,2048]{3,2,1,0:T(8,128)(2,1)S(1)}, u32[]{:S(2)}, u32[]{:S(2)}) %all-to-all-start.1) | async-done | bytes 1048608 | tf_op jit(solution)/shard_map/all_to_all | solution.py:37
  122.5 0.1 maximum_bitcast_fusion
  122.7 0.2 copy.17
  122.9 0.6 copy.22
  123.5 0.5 copy.24
  124.1 0.1 slice_bitcast_fusion
  124.2 0.8 gather_fusion
  125.1 1.9 gather_fusion.1
  127.0 3.3 %convolution_multiply_fusion.1 = f32[20,256,128]{2,1,0:T(8,128)} fusion(bf16[20,256,128]{2,1,0:T(8,128)(2,1)S(1)} %gather_fusion, f32[20]{0:T(128)S(1)} %copy-done.4, bf16[2,1,1,20,128,128]{5,4,3,2,1,0:T(8,128)(2,1)} %param.8), kind=kOutput, calls=%fused_computation.8 | convolution fusion | flops 168427520 | bytes 4587600 | tf_op jit(solution)/shard_map/bfk,brk->bfr/dot_general | solution.py:48
  130.3 0.5 convolution_multiply_fusion
  130.8 3.4 %broadcast_in_dim.7 = f32[48,256,128]{2,1,0:T(8,128)} broadcast(f32[]{:T(128)} %constant.4.clone.1), dimensions={} | broadcast | bytes 6291460 | tf_op jit(solution)/shard_map/broadcast_in_dim | solution.py:63
  134.2 9.5 %scatter_fusion = f32[48,256,128]{2,1,0:T(8,128)} fusion(f32[48,256,128]{2,1,0:T(8,128)} %broadcast_in_dim.7, s32[20]{0:T(128)S(1)} %get-tuple-element.12, f32[20,256,128]{2,1,0:T(8,128)} %convolution_multiply_fusion.1), kind=kCustom, calls=%fused_computation.2 | custom fusion | flops 655360 | bytes 7864400 | tf_op jit(solution)/shard_map/scatter-add | solution.py:49
  143.7 8.5 %scatter_fusion.1 = f32[48,256,128]{2,1,0:T(8,128)} fusion(f32[48,256,128]{2,1,0:T(8,128)} %scatter_fusion, s32[20]{0:T(128)S(1)} %get-tuple-element.11, f32[20,256,128]{2,1,0:T(8,128)S(1)} %convolution_multiply_fusion), kind=kCustom, calls=%fused_computation.3 | custom fusion | flops 655360 | bytes 7864400 | tf_op jit(solution)/shard_map/scatter-add | solution.py:49
  152.2 0.0 reduce-scatter.3.cloned.1.call-update
  152.2 0.0 reduce-scatter.5.cloned.1.call-start
  152.3 73.0 %reduce-scatter.3.cloned.1.call-done = f32[6,256,128]{2,1,0:T(8,128)} async-done(((f32[48,256,128]{2,1,0:T(8,128)}), f32[6,256,128]{2,1,0:T(8,128)}) %reduce-scatter.3.cloned.1.call-update) | async-done | bytes 786448 | tf_op jit(solution)/shard_map/reduce_scatter | solution.py:43
  225.3 25.1 %reduce-scatter.5.cloned.1.call-done = f32[3,256,128]{2,1,0:T(8,128)} async-done(((f32[6,256,128]{2,1,0:T(8,128)}), f32[3,256,128]{2,1,0:T(8,128)}) %reduce-scatter.5.cloned.1.call-update) | async-done | bytes 393232 | tf_op jit(solution)/shard_map/reduce_scatter | solution.py:43
  250.4 1.2 fusion.6
  251.7 0.7 fusion.5
  (25 shorter events, 0.1 us)
Async XLA Ops:
  6.5 243.9 %copy-start = (bf16[256,256]{1,0:T(8,128)(2,1)S(1)}, bf16[256,256]{1,0:T(8,128)(2,1)}, u32[]{:S(2)}) copy-start(bf16[256,256]{1,0:T(8,128)(2,1)} %param.14) | copy-start | bytes 393220
  6.5 43.1 %all-gather.2.cloned.1.call-start = ((), (), s32[]{:S(2)}) async-start(), calls=%async_computation.4 | async-start | bytes 2228224 | tf_op jit(solution)/shard_map/all_gather | solution.py:60
  54.4 36.2 %all-to-all-start = ((bf16[16,2,8,2048]{3,2,1,0:T(8,128)(2,1)}), bf16[16,2,8,2048]{3,2,1,0:T(8,128)(2,1)S(1)}, u32[]{:S(2)}, u32[]{:S(2)}) async-start(bf16[16,2,8,2048]{3,2,1,0:T(8,128)(2,1)} %copy.15), calls=%async_computation | async-start | bytes 2097152 | tf_op jit(solution)/shard_map/all_to_all | solution.py:37
  63.3 33.2 %copy-start.6 = (s32[2,1,1]{0,2,1:T(1,128)S(1)}, s32[2,1,1]{0,2,1:T(1,128)}, u32[]{:S(2)}) copy-start(s32[2,1,1]{0,2,1:T(1,128)} %param.11) | copy-start | bytes 28
  63.3 33.8 %copy-start.8 = (s32[2,1,1,20]{3,2,1,0:T(1,128)S(1)}, s32[2,1,1,20]{3,2,1,0:T(1,128)}, u32[]{:S(2)}) copy-start(s32[2,1,1,20]{3,2,1,0:T(1,128)} %param.10) | copy-start | bytes 484
  63.3 33.8 %copy-start.9 = (s32[2,1,1,20]{3,2,1,0:T(1,128)S(1)}, s32[2,1,1,20]{3,2,1,0:T(1,128)}, u32[]{:S(2)}) copy-start(s32[2,1,1,20]{3,2,1,0:T(1,128)} %param.9) | copy-start | bytes 484
  63.3 33.8 %copy-start.5 = (bf16[2,1,1,20]{3,0,2,1:T(2,128)(2,1)S(1)}, bf16[2,1,1,20]{3,0,2,1:T(2,128)(2,1)}, u32[]{:S(2)}) copy-start(bf16[2,1,1,20]{3,0,2,1:T(2,128)(2,1)} %param.12) | copy-start | bytes 244
  90.5 32.0 %all-to-all-start.1 = ((bf16[16,2,8,2048]{3,2,1,0:T(8,128)(2,1)}), bf16[16,2,8,2048]{3,2,1,0:T(8,128)(2,1)S(1)}, u32[]{:S(2)}, u32[]{:S(2)}) async-start(bf16[16,2,8,2048]{3,2,1,0:T(8,128)(2,1)} %copy.16), calls=%async_computation.1 | async-start | bytes 2097152 | tf_op jit(solution)/shard_map/all_to_all | solution.py:37
  96.5 128.8 %reduce-scatter.3.cloned.1.call-start = ((), (), s32[]{:S(2)}) async-start(), calls=%async_computation.5 | async-start | bytes 7077888 | tf_op jit(solution)/shard_map/reduce_scatter | solution.py:43
  125.0 1.9 copy-start.4
  126.9 3.3 %copy-start.1 = (bf16[20,256,128]{2,1,0:T(8,128)(2,1)S(1)}, bf16[20,256,128]{2,1,0:T(8,128)(2,1)}, u32[]{:S(2)}) copy-start(bf16[20,256,128]{2,1,0:T(8,128)(2,1)} %gather_fusion.1) | copy-start | bytes 3932164
  126.9 3.3 %copy-start.2 = (bf16[2,1,1,20,128,128]{5,4,3,2,1,0:T(8,128)(2,1)S(1)}, bf16[2,1,1,20,128,128]{5,4,3,2,1,0:T(8,128)(2,1)}, u32[]{:S(2)}) copy-start(bf16[2,1,1,20,128,128]{5,4,3,2,1,0:T(8,128)(2,1)} %param.8) | copy-start | bytes 3932164
  127.0 3.3 %copy-start.3 = (f32[20]{0:T(128)S(1)}, f32[20]{0:T(128)}, u32[]{:S(2)}) copy-start(f32[20]{0:T(128)} %get-tuple-element.13) | copy-start | bytes 244
  152.2 99.4 %copy-start.7 = (f32[256]{0:T(256)S(1)}, f32[256]{0:T(256)}, u32[]{:S(2)}) copy-start(f32[256]{0:T(256)} %param.15) | copy-start | bytes 3076
  152.2 98.2 %reduce-scatter.5.cloned.1.call-start = ((), (), s32[]{:S(2)}) async-start(), calls=%async_computation.6 | async-start | bytes 1179648 | tf_op jit(solution)/shard_map/reduce_scatter | solution.py:43
Sparse Core Ops, SparseCore 0:
  9.1 40.4 all-gather.1
  152.4 72.8 reduce-scatter.2
  227.7 22.5 reduce-scatter.4
where the time goes:
time: 259 us
  waiting for transfers between devices  190 us (73%)
  other arithmetic  20.7 us (8%)
  starting transfers between devices  14.9 us (6%)
  local copies, waits for them, and re-layouts  14.5 us (6%)
  between operations  13.3 us (5%)
  matrix products  5.03 us (2%)
    reduce_scatter x2, waiting for transfers between devices, scatter_axes(): x = lax.psum_scatter(x, axis, scatter_dimension=dim, tiled=True)  98.1 us
    all_to_all x2, waiting for transfers between devices, several_exchanges(): lax.all_to_all(share, axis, split_axis=0, concat_axis=0, tiled=True)  49.2 us
    all_gather x1, waiting for transfers between devices, body(): panels = lax.all_gather(panel_features, 'row', axis=2, tiled=True)  42.4 us
    scatter-add x2, other arithmetic, spread_rows(): return running.at[row_ids].add(contrib * live_scale[:, None, None])  18 us
    all_to_all x2, starting transfers between devices, several_exchanges(): lax.all_to_all(share, axis, split_axis=0, concat_axis=0, tiled=True)  14.8 us
  transfers between devices with their start and end apart: 5, of which 5 were waited for; matrix products, arithmetic and copies ran while one was open for 2% of the time, Pallas kernels for 0%

commit v1 on v0

--- a/solution.py
+++ b/solution.py
@@ -8,6 +8,11 @@
 PCB = 16
 COL = ("col_0", "col_1")
 ROW_COL = ("row", "col_0", "col_1")
+
+
+def swapped_in(x, axis, along):
+    sent = jnp.stack([x] * lax.axis_size(axis))
+    return jnp.concatenate(lax.all_to_all(sent, axis, 0, 0), axis=along)
 
 
 def in_blocks(x, dim, peers):
@@ -57,7 +62,7 @@
     feat_all = weight.shape[0]
     out_width = weight.shape[1]
     rows_here = ROWB_DEV * blocksz // lax.axis_size(COL)
-    panels = lax.all_gather(panel_features, "row", axis=2, tiled=True)
+    panels = swapped_in(panel_features, "row", 2)
     shares = several_exchanges(panels, COL, 2, 2, 1)
     share_blocks = shares.reshape(nsteps, feat_all, PCB, blocksz).transpose(0, 2, 1, 3)
     running = jnp.zeros((ROWB_DEV, feat_all, blocksz), jnp.float32)

time: 259 us -> 249 us (0.961)
  blocking collectives: 0 us -> 71.7 us
  waiting for transfers between devices: 190 us -> 123 us
  starting transfers between devices: 14.9 us -> 4.4 us
  local copies, waits for them, and re-layouts: 14.5 us -> 10.6 us
    all_to_all x0 -> x2, blocking collectives: none -> 71.7 us  [the longest x1 38.5 us: several_exchanges(): lax.all_to_all(share, axis, split_axis=0, concat_axis=0, tiled=True)]
    all_gather x1 -> x0, waiting for transfers between devices: 42.4 us -> none  [body(): panels = lax.all_gather(panel_features, 'row', axis=2, tiled=True)]
    all_to_all x2 -> x1, waiting for transfers between devices: 49.2 us -> 23.6 us  [several_exchanges(): lax.all_to_all(share, axis, split_axis=0, concat_axis=0, tiled=True)]
    all_to_all x2 -> x1, starting transfers between devices: 14.8 us -> 4.32 us  [several_exchanges(): lax.all_to_all(share, axis, split_axis=0, concat_axis=0, tiled=True)]
    unnamed x22 -> x21, local copies, waits for them, and re-layouts: 3.42 us -> 0.67 us
  transfers between devices with their start and end apart: 5 -> 3, of which waited for: 5 -> 3; matrix products, arithmetic and copies ran while one was open for 2% -> 1% of each run, Pallas kernels for 0% -> 0%
where the time goes in v1:
time: 249 us; the launch traced here: 248 us
  waiting for transfers between devices  123 us (49%)
  blocking collectives  71.7 us (29%)
  other arithmetic  20.4 us (8%)
  between operations  13.6 us (5%)
  local copies, waits for them, and re-layouts  10.6 us (4%)
  matrix products  5.04 us (2%)
  starting transfers between devices  4.4 us (2%)
    reduce_scatter x2, waiting for transfers between devices, scatter_axes(): x = lax.psum_scatter(x, axis, scatter_dimension=dim, tiled=True)  98.9 us
    all_to_all x1, blocking collectives, several_exchanges(): lax.all_to_all(share, axis, split_axis=0, concat_axis=0, tiled=True)  38.5 us
    all_to_all x1, blocking collectives, swapped_in(): return jnp.concatenate(lax.all_to_all(sent, axis, 0, 0), axis=along)  33.2 us
    all_to_all x1, waiting for transfers between devices, several_exchanges(): lax.all_to_all(share, axis, split_axis=0, concat_axis=0, tiled=True)  23.6 us
    scatter-add x2, other arithmetic, spread_rows(): return running.at[row_ids].add(contrib * live_scale[:, None, None])  17.8 us
  transfers between devices with their start and end apart: 3, of which 3 were waited for; matrix products, arithmetic and copies ran while one was open for 1% of the time, Pallas kernels for 0%

profile of v1, /device:TPU:1, one launch (start us, length us, event | category | flops | bytes accessed | tf_op | source)
XLA Modules:
  0.0 248.2 jit_solution(5152177760272052376)
XLA Ops:
  6.5 0.0 copy-start
  6.5 1.2 stack.2
  7.7 33.2 %all_to_all.15 = bf16[16,2,16,2048]{3,2,1,0:T(8,128)(2,1)S(1)} all-to-all(bf16[16,2,16,2048]{3,2,1,0:T(8,128)(2,1)S(1)} %stack.2), channel_id=1, replica_groups=mesh['row'=16,'col_0'=8,'col_1'=2] {'row'}, dimensions={0} | all-to-all | bytes 4194304 | tf_op jit(solution)/shard_map/all_to_all | solution.py:15
  40.9 1.2 fusion.13
  42.1 38.5 %all_to_all.16 = bf16[16,2,8,2048]{3,2,1,0:T(8,128)(2,1)S(1)} all-to-all(bf16[16,2,8,2048]{3,2,1,0:T(8,128)(2,1)S(1)} %get-tuple-element.7), channel_id=1, replica_groups=mesh['row'=16,'col_0'=8,'col_1'=2] {'col_0','col_1'}, dimensions={0} | all-to-all | bytes 2097152 | tf_op jit(solution)/shard_map/all_to_all | solution.py:42
  80.6 4.3 %all-to-all-start.2 = ((bf16[16,2,8,2048]{3,2,1,0:T(8,128)(2,1)}), bf16[16,2,8,2048]{3,2,1,0:T(8,128)(2,1)S(1)}, u32[]{:S(2)}, u32[]{:S(2)}) async-start(bf16[16,2,8,2048]{3,2,1,0:T(8,128)(2,1)} %get-tuple-element.8), calls=%async_computation.2 | async-start | bytes 2097152 | tf_op jit(solution)/shard_map/all_to_all | solution.py:42
  84.9 0.0 reduce-scatter.3.cloned.1.call-start
  85.0 0.6 fusion.14
  85.6 1.7 compare_select_fusion.4
  87.4 23.6 %all-to-all-done.2 = bf16[16,2,8,2048]{3,2,1,0:T(8,128)(2,1)S(1)} async-done(((bf16[16,2,8,2048]{3,2,1,0:T(8,128)(2,1)}), bf16[16,2,8,2048]{3,2,1,0:T(8,128)(2,1)S(1)}, u32[]{:S(2)}, u32[]{:S(2)}) %all-to-all-start.2) | async-done | bytes 1048608 | tf_op jit(solution)/shard_map/all_to_all | solution.py:42
  110.9 0.1 maximum_bitcast_fusion
  111.1 0.2 copy.11
  111.3 0.6 copy.15
  112.0 0.5 copy.17
  112.5 0.1 slice_bitcast_fusion
  112.7 0.8 gather_fusion
  113.5 0.0 copy-start.4
  113.5 1.9 gather_fusion.1
  115.4 3.3 %convolution_multiply_fusion.1 = f32[20,256,128]{2,1,0:T(8,128)} fusion(bf16[20,256,128]{2,1,0:T(8,128)(2,1)S(1)} %gather_fusion, f32[20]{0:T(128)S(1)} %copy-done.4, bf16[2,1,1,20,128,128]{5,4,3,2,1,0:T(8,128)(2,1)} %param.8), kind=kOutput, calls=%fused_computation.7 | convolution fusion | flops 168427520 | bytes 4587600 | tf_op jit(solution)/shard_map/bfk,brk->bfr/dot_general | solution.py:53
  118.7 0.0 copy-done.2
  118.7 0.5 convolution_multiply_fusion
  119.2 3.4 %broadcast_in_dim.7 = f32[48,256,128]{2,1,0:T(8,128)} broadcast(f32[]{:T(128)} %constant.4.clone.1), dimensions={} | broadcast | bytes 6291460 | tf_op jit(solution)/shard_map/broadcast_in_dim | solution.py:68
  122.6 9.3 %scatter_fusion = f32[48,256,128]{2,1,0:T(8,128)} fusion(f32[48,256,128]{2,1,0:T(8,128)} %broadcast_in_dim.7, s32[20]{0:T(128)S(1)} %get-tuple-element.12, f32[20,256,128]{2,1,0:T(8,128)} %convolution_multiply_fusion.1), kind=kCustom, calls=%fused_computation.2 | custom fusion | flops 655360 | bytes 7864400 | tf_op jit(solution)/shard_map/scatter-add | solution.py:54
  131.9 8.5 %scatter_fusion.1 = f32[48,256,128]{2,1,0:T(8,128)} fusion(f32[48,256,128]{2,1,0:T(8,128)} %scatter_fusion, s32[20]{0:T(128)S(1)} %get-tuple-element.11, f32[20,256,128]{2,1,0:T(8,128)S(1)} %convolution_multiply_fusion), kind=kCustom, calls=%fused_computation.3 | custom fusion | flops 655360 | bytes 7864400 | tf_op jit(solution)/shard_map/scatter-add | solution.py:54
  140.4 0.0 reduce-scatter.3.cloned.1.call-update
  140.4 0.0 reduce-scatter.5.cloned.1.call-start
  140.5 73.8 %reduce-scatter.3.cloned.1.call-done = f32[6,256,128]{2,1,0:T(8,128)} async-done(((f32[48,256,128]{2,1,0:T(8,128)}), f32[6,256,128]{2,1,0:T(8,128)}) %reduce-scatter.3.cloned.1.call-update) | async-done | bytes 786448 | tf_op jit(solution)/shard_map/reduce_scatter | solution.py:48
  214.3 0.0 reduce-scatter.5.cloned.1.call-update
  214.3 25.1 %reduce-scatter.5.cloned.1.call-done = f32[3,256,128]{2,1,0:T(8,128)} async-done(((f32[6,256,128]{2,1,0:T(8,128)}), f32[3,256,128]{2,1,0:T(8,128)}) %reduce-scatter.5.cloned.1.call-update) | async-done | bytes 393232 | tf_op jit(solution)/shard_map/reduce_scatter | solution.py:48
  239.4 1.2 fusion.6
  240.7 0.0 copy-done.7
  240.7 0.7 fusion.5
  (19 shorter events, 0.0 us)
Async XLA Ops:
  6.5 232.9 %copy-start = (bf16[256,256]{1,0:T(8,128)(2,1)S(1)}, bf16[256,256]{1,0:T(8,128)(2,1)}, u32[]{:S(2)}) copy-start(bf16[256,256]{1,0:T(8,128)(2,1)} %param.14) | copy-start | bytes 393220
  42.1 42.9 %copy-start.6 = (s32[2,1,1]{0,2,1:T(1,128)S(1)}, s32[2,1,1]{0,2,1:T(1,128)}, u32[]{:S(2)}) copy-start(s32[2,1,1]{0,2,1:T(1,128)} %param.11) | copy-start | bytes 28
  42.1 43.5 %copy-start.8 = (s32[2,1,1,20]{3,2,1,0:T(1,128)S(1)}, s32[2,1,1,20]{3,2,1,0:T(1,128)}, u32[]{:S(2)}) copy-start(s32[2,1,1,20]{3,2,1,0:T(1,128)} %param.10) | copy-start | bytes 484
  42.1 43.5 %copy-start.9 = (s32[2,1,1,20]{3,2,1,0:T(1,128)S(1)}, s32[2,1,1,20]{3,2,1,0:T(1,128)}, u32[]{:S(2)}) copy-start(s32[2,1,1,20]{3,2,1,0:T(1,128)} %param.9) | copy-start | bytes 484
  42.1 43.5 %copy-start.5 = (bf16[2,1,1,20]{3,0,2,1:T(2,128)(2,1)S(1)}, bf16[2,1,1,20]{3,0,2,1:T(2,128)(2,1)}, u32[]{:S(2)}) copy-start(bf16[2,1,1,20]{3,0,2,1:T(2,128)(2,1)} %param.12) | copy-start | bytes 244
  80.6 30.3 %all-to-all-start.2 = ((bf16[16,2,8,2048]{3,2,1,0:T(8,128)(2,1)}), bf16[16,2,8,2048]{3,2,1,0:T(8,128)(2,1)S(1)}, u32[]{:S(2)}, u32[]{:S(2)}) async-start(bf16[16,2,8,2048]{3,2,1,0:T(8,128)(2,1)} %get-tuple-element.8), calls=%async_computation.2 | async-start | bytes 2097152 | tf_op jit(solution)/shard_map/all_to_all | solution.py:42
  84.9 129.3 %reduce-scatter.3.cloned.1.call-start = ((), (), s32[]{:S(2)}) async-start(), calls=%async_computation.5 | async-start | bytes 7077888 | tf_op jit(solution)/shard_map/reduce_scatter | solution.py:48
  113.5 1.9 copy-start.4
  115.3 3.3 %copy-start.1 = (bf16[20,256,128]{2,1,0:T(8,128)(2,1)S(1)}, bf16[20,256,128]{2,1,0:T(8,128)(2,1)}, u32[]{:S(2)}) copy-start(bf16[20,256,128]{2,1,0:T(8,128)(2,1)} %gather_fusion.1) | copy-start | bytes 3932164
  115.3 3.3 %copy-start.2 = (bf16[2,1,1,20,128,128]{5,4,3,2,1,0:T(8,128)(2,1)S(1)}, bf16[2,1,1,20,128,128]{5,4,3,2,1,0:T(8,128)(2,1)}, u32[]{:S(2)}) copy-start(bf16[2,1,1,20,128,128]{5,4,3,2,1,0:T(8,128)(2,1)} %param.8) | copy-start | bytes 3932164
  115.3 3.3 %copy-start.3 = (f32[20]{0:T(128)S(1)}, f32[20]{0:T(128)}, u32[]{:S(2)}) copy-start(f32[20]{0:T(128)} %get-tuple-element.13) | copy-start | bytes 244
  140.4 100.3 %copy-start.7 = (f32[256]{0:T(256)S(1)}, f32[256]{0:T(256)}, u32[]{:S(2)}) copy-start(f32[256]{0:T(256)} %param.15) | copy-start | bytes 3076
  140.4 99.0 %reduce-scatter.5.cloned.1.call-start = ((), (), s32[]{:S(2)}) async-start(), calls=%async_computation.6 | async-start | bytes 1179648 | tf_op jit(solution)/shard_map/reduce_scatter | solution.py:48
Sparse Core Ops, SparseCore 0:
  140.5 73.6 reduce-scatter.2
  216.8 22.5 reduce-scatter.4
